TPU v7x, 128 devices: a whole 4x4x4 slice. The times are simulated.
128 devices in a mesh: rep: 16 (over x, z), own: 8 (over y, core).
Axes of the slice: x: 4, y: 4, z: 4, core: 2. Of those that a mesh axis runs over, the one named last changes fastest.
Arguments:
- grads: bfloat16 [16, 8, 3, 768, 768], P('rep', 'own'), may hold values from -0.059814453 to 0.059814453
- weights: float32 [3, 768, 768], P(None, 'own'), may hold values from -0.21875 to 0.21875
- mom_first: float32 [3, 768, 768], P(None, 'own'), may hold values from -3 to 3
- mom_second: float32 [3, 768, 768], P(None, 'own'), may hold values from 0.003 to 0.03
- left_stat: float32 [8, 768, 768], P('own'), may hold values from -3 to 33, as said below
- right_stat: float32 [8, 768, 768], P('own'), may hold values from -3 to 33, as said below
- left_root: float32 [8, 768, 768], P('own'), may hold values from -1 to 4, as said below
- right_root: float32 [8, 768, 768], P('own'), may hold values from -1 to 4, as said below
- owners: int32 [3], replicated, may hold values from 0 to 7, as said below
Outputs:
- new_weights: float32 [3, 768, 768], P(None, 'own')
- new_mom_first: float32 [3, 768, 768], P(None, 'own')
- new_mom_second: float32 [3, 768, 768], P(None, 'own')
- new_left: float32 [8, 768, 768], P('own')
- new_right: float32 [8, 768, 768], P('own')
Inputs may be any that keep to these rules, and one draw needn't show every extreme that they name: `owners`: the 3 entries are distinct, and one of them is always 8 - 1. `left_stat`: each slot is symmetric. `right_stat`: each slot is symmetric. `left_root`: each slot is symmetric. `right_root`: each slot is symmetric.
All inputs are finite; a program needn't handle non-finite values.
Results may differ from a plain program's by a relative error of at most 0.008.
Values may be sent and summed in bfloat16 or wider, within the bound.
A program may use at most 128 MiB of HBM per device.

v0:
```python
import jax
import jax.numpy as jnp
from jax import lax
from jax.sharding import PartitionSpec as P

first_decay = 0.9
second_decay = 0.95
adam_epsilon = 1e-08
graft_floor = 1e-06
learn_rate = 0.05


def broadcast(shard, axis, root):
    mine = lax.axis_index(axis) == root
    return lax.psum(jnp.where(mine, shard, jnp.zeros_like(shard)), axis)


def on_device(
    grads, weights, mom_first, mom_second, left_stat, right_stat, left_root, right_root, owners
):
    own_index = lax.axis_index("own")
    row_count = weights.shape[1]
    row_start = own_index * row_count
    width = weights.shape[2]
    local_grad = grads[0, 0].astype(jnp.float32)
    matched = owners == own_index
    holding = jnp.any(matched)
    item_index = jnp.sum(jnp.where(matched, jnp.arange(owners.shape[0], dtype=jnp.int32), 0))
    summed = lax.psum(local_grad, ("rep", "own")).astype(jnp.bfloat16)
    my_rows = lax.dynamic_slice_in_dim(summed, row_start, row_count, 1)
    picked = lax.dynamic_index_in_dim(summed, item_index, 0, keepdims=False)
    grad_mat = jnp.where(holding, picked, jnp.zeros_like(picked))
    wide_rows = my_rows.astype(jnp.float32)
    first_new = first_decay * mom_first + (1.0 - first_decay) * wide_rows
    second_new = second_decay * mom_second + (1.0 - second_decay) * wide_rows * wide_rows
    adam_step = first_new / (jnp.sqrt(second_new) + adam_epsilon)
    partial_squares = jnp.sum(adam_step * adam_step, axis=(1, 2))
    adam_total = lax.psum(partial_squares, "own")
    adam_mean = jnp.sum(jnp.where(matched, adam_total, 0.0)) / (width * width)
    left_new = left_stat[0] + jnp.einsum(
        "ik,jk->ij", grad_mat, grad_mat, preferred_element_type=jnp.float32
    )
    right_new = right_stat[0] + jnp.einsum(
        "ki,kj->ij", grad_mat, grad_mat, preferred_element_type=jnp.float32
    )
    half_product = jnp.dot(
        left_root[0], grad_mat.astype(jnp.float32), precision=lax.Precision.HIGHEST
    )
    direction = jnp.dot(half_product, right_root[0], precision=lax.Precision.HIGHEST)
    graft_scale = jnp.sqrt(adam_mean / (jnp.mean(direction * direction) + graft_floor))
    update = graft_scale * direction
    pieces = []
    for position in range(owners.shape[0]):
        full_update = broadcast(update, "own", owners[position])
        pieces.append(lax.dynamic_slice_in_dim(full_update, row_start, row_count, 0))
    my_update = jnp.stack(pieces)
    new_weights = weights - learn_rate * my_update
    return (new_weights, first_new, second_new, left_new[None], right_new[None])


def solution(mesh):
    placed = (
        P("rep", "own", None, None, None),
        P(None, "own", None),
        P(None, "own", None),
        P(None, "own", None),
        P("own", None, None),
        P("own", None, None),
        P("own", None, None),
        P("own", None, None),
        P(),
    )
    return jax.shard_map(
        on_device,
        mesh=mesh,
        in_specs=placed,
        out_specs=(
            P(None, "own", None),
            P(None, "own", None),
            P(None, "own", None),
            P("own", None, None),
            P("own", None, None),
        ),
        check_vma=False,
    )
```

profile of v0, /device:TPU:1, one launch (start us, length us, event | category | flops | bytes accessed | tf_op | source)
XLA Modules:
  0.0 268.5 jit_solution(13074757025672226262)
XLA Ops:
  7.2 0.0 copy-start
  7.2 0.0 all-reduce.4.cloned.1.call-start
  7.2 1.5 fusion.21
  8.7 1.3 select_reduce_fusion
  10.0 1.4 fusion.24
  14.6 5.5 %bitcast_convert_fusion = f32[3,768,768]{2,1,0:T(8,128)} fusion(bf16[1,1,3,768,768]{4,3,2,1,0:T(8,128)(2,1)} %param.9), kind=kLoop, calls=%fused_computation | loop fusion | flops 1769472 | bytes 10616832 | tf_op jit(solution)/shard_map/convert_element_type | solution.py:25
  20.1 0.0 copy-start.1
  20.1 111.3 %all-reduce.5 = bf16[3,768,768]{2,1,0:T(8,128)(2,1)} all-reduce(f32[3,768,768]{2,1,0:T(8,128)} %bitcast_convert_fusion), channel_id=1, replica_groups=mesh['rep'=16,'own'=8] {'rep','own'}, use_global_device_ids=true, to_apply=%region_0.0 | all-reduce | flops 1769472 | bytes 10616832 | tf_op jit(solution)/shard_map/psum | solution.py:29
  131.5 0.0 copy-start.3
  131.5 0.0 copy-done.1
  131.5 3.1 %multiply_reduce_fusion.1 = (f32[3]{0:T(128)S(1)}, f32[3,96,768]{2,1,0:T(8,128)}, f32[3,96,768]{2,1,0:T(8,128)}) fusion(bf16[3,768,768]{2,1,0:T(8,128)(2,1)} %all-reduce.5, s32[]{:T(128)S(6)} %select_n.54, f32[3,96,768]{2,1,0:T(8,128)S(1)} %copy-done.1, f32[3,96,768]{2,1,0:T(8,128)} %param.11), kind=kLoop, calls=%fused_computation.23 | loop fusion | flops 2654205 | bytes 3981328 | tf_op jit(solution)/shard_map/reduce_sum | solution.py:37
  134.6 14.5 %psum.36 = f32[3]{0:T(128)S(1)} all-reduce(f32[3]{0:T(128)S(1)} %get-tuple-element.8), channel_id=1, replica_groups=mesh['rep'=16,'own'=8] {'own'}, use_global_device_ids=true, to_apply=%region_2.3 | all-reduce | flops 3 | bytes 24 | tf_op jit(solution)/shard_map/psum | solution.py:38
  149.1 0.0 copy-done.3
  149.1 0.6 select_reduce_fusion.1
  151.0 6.2 %fusion.4 = f32[768,768]{1,0:T(8,128)S(1)} fusion(f32[1,768,768]{2,1,0:T(8,128)} %param.15, bf16[3,768,768]{2,1,0:T(8,128)(2,1)} %all-reduce.5, s32[]{:T(128)S(6)} %select_n.58, pred[]{:T(512)} %fusion.21), kind=kOutput, calls=%fused_computation.7 | convolution fusion | flops 5436407808 | bytes 5898756 | tf_op jit(solution)/shard_map/dot_general | solution.py:46
  157.2 0.0 copy-done
  157.2 8.6 %multiply_reduce_fusion = (f32[]{:T(128)}, f32[768,768]{1,0:T(8,128)}) fusion(f32[768,768]{1,0:T(8,128)S(1)} %fusion.4, f32[1,768,768]{2,1,0:T(8,128)S(1)} %copy-done), kind=kOutput, calls=%fused_computation.9 | convolution fusion | flops 5436997632 | bytes 7077892 | tf_op jit(solution)/shard_map/dot_general | solution.py:49
  166.5 4.8 %multiply_select_fusion.2 = (f32[768,768]{1,0:T(8,128)}, f32[768,768]{1,0:T(8,128)}, f32[768,768]{1,0:T(8,128)}) fusion(f32[768,768]{1,0:T(8,128)} %get-tuple-element.18, f32[]{:T(128)S(6)} %sqrt.7, pred[]{:T(512)S(6)} %eq.15, pred[]{:T(512)S(6)} %eq.18, pred[]{:T(512)S(6)} %eq.19), kind=kLoop, calls=%fused_computation.12 | loop fusion | flops 2359296 | bytes 9437191 | tf_op jit(solution)/shard_map/jit(_where)/select_n | solution.py:15
  171.3 0.0 all-reduce.4.cloned.1.call-update
  171.3 0.0 copy-start.4
  171.3 5.7 %fusion.1 = f32[1,768,768]{2,1,0:T(8,128)} fusion(f32[1,768,768]{2,1,0:T(8,128)} %param.13, bf16[3,768,768]{2,1,0:T(8,128)(2,1)} %all-reduce.5, s32[]{:T(128)S(6)} %select_n.58, pred[]{:T(512)} %fusion.21), kind=kOutput, calls=%fused_computation.4 | convolution fusion | flops 907149312 | bytes 5898756 | tf_op jit(solution)/shard_map/ik,jk->ij/dot_general | solution.py:40
  177.1 0.0 copy-done.4
  177.1 4.9 %fusion = f32[1,768,768]{2,1,0:T(8,128)} fusion(f32[1,768,768]{2,1,0:T(8,128)S(1)} %copy-done.4, bf16[3,768,768]{2,1,0:T(8,128)(2,1)} %all-reduce.5, s32[]{:T(128)S(6)} %select_n.58, pred[]{:T(512)} %fusion.21), kind=kOutput, calls=%fused_computation.2 | convolution fusion | flops 907149312 | bytes 5898756 | tf_op jit(solution)/shard_map/ki,kj->ij/dot_general | solution.py:43
  182.0 0.0 copy-start.2
  182.0 76.5 %all-reduce.4.cloned.1.call-done = (f32[768,768]{1,0:T(8,128)}, f32[768,768]{1,0:T(8,128)}, f32[768,768]{1,0:T(8,128)}) async-done(((f32[768,768]{1,0:T(8,128)}, f32[768,768]{1,0:T(8,128)}, f32[768,768]{1,0:T(8,128)}), (f32[768,768]{1,0:T(8,128)}, f32[768,768]{1,0:T(8,128)}, f32[768,768]{1,0:T(8,128)})) %all-reduce.4.cloned.1.call-update) | async-done | bytes 7077904 | tf_op jit(solution)/shard_map/psum | solution.py:15
  258.5 1.0 dynamic-slice_bitcast_fusion.2
  259.5 1.1 dynamic-slice_bitcast_fusion
  260.6 0.0 copy-done.2
  260.6 1.0 fusion.11
Async XLA Ops:
  7.2 150.1 %copy-start = (f32[1,768,768]{2,1,0:T(8,128)S(1)}, f32[1,768,768]{2,1,0:T(8,128)}, u32[]{:S(2)}) copy-start(f32[1,768,768]{2,1,0:T(8,128)} %param.16) | copy-start | bytes 7077892
  7.2 251.3 %all-reduce.4.cloned.1.call-start = ((), (), s32[]{:S(2)}) async-start(), calls=%async_computation | async-start | bytes 14155776 | tf_op jit(solution)/shard_map/psum | solution.py:15
  20.1 111.3 %copy-start.1 = (f32[3,96,768]{2,1,0:T(8,128)S(1)}, f32[3,96,768]{2,1,0:T(8,128)}, u32[]{:S(2)}) copy-start(f32[3,96,768]{2,1,0:T(8,128)} %param.12) | copy-start | bytes 2654212
  131.5 17.6 %copy-start.3 = (s32[3]{0:T(128)S(1)}, s32[3]{0:T(128)}, u32[]{:S(2)}) copy-start(s32[3]{0:T(128)} %param.17) | copy-start | bytes 40
  171.3 5.8 %copy-start.4 = (f32[1,768,768]{2,1,0:T(8,128)S(1)}, f32[1,768,768]{2,1,0:T(8,128)}, u32[]{:S(2)}) copy-start(f32[1,768,768]{2,1,0:T(8,128)} %param.14) | copy-start | bytes 7077892
  182.0 78.6 %copy-start.2 = (f32[3,96,768]{2,1,0:T(8,128)S(1)}, f32[3,96,768]{2,1,0:T(8,128)}, u32[]{:S(2)}) copy-start(f32[3,96,768]{2,1,0:T(8,128)} %param.10) | copy-start | bytes 2654212
Sparse Core Ops, SparseCore 0:
  171.4 87.0 all-reduce.3
where the time goes:
time: 269 us; the launch traced here: 268 us
  blocking collectives  126 us (47%)
  waiting for transfers between devices  76.5 us (28%)
  matrix products  25.4 us (9%)
  between operations  19.4 us (7%)
  other arithmetic  17.8 us (7%)
  local copies, waits for them, and re-layouts  3.46 us (1%)
    psum x1, blocking collectives, on_device(): summed = lax.psum(local_grad, ('rep', 'own')).astype(jnp.bfloat16)  111 us
    psum x1, waiting for transfers between devices, broadcast(): return lax.psum(jnp.where(mine, shard, jnp.zeros_like(shard)), axis)  76.5 us
    psum x1, blocking collectives, on_device(): adam_total = lax.psum(partial_squares, 'own')  14.5 us
    dot_general x1, matrix products, on_device(): jnp.dot(half_product, right_root[0], precision=lax.Precision.HIGHEST)  8.55 us
    dot_general x1, matrix products, on_device(): jnp.dot(left_root[0], grad_mat.astype(jnp.float32), precision=lax.Precisi...  6.22 us
    dot_general x1, matrix products, on_device(): jnp.einsum('ik,jk->ij', grad_mat, grad_mat, preferred_element_type=jnp.fl...  5.74 us
    convert_element_type x1, other arithmetic, on_device(): local_grad = grads[0, 0].astype(jnp.float32)  5.52 us
  transfers between devices with their start and end apart: 1, of which 1 were waited for; matrix products, arithmetic and copies ran while one was open for 4% of the time, Pallas kernels for 0%

commit v1 on v0

v1 whole, which is shorter than its diff:
```python
import functools

import jax
import jax.numpy as jnp
from jax import lax
from jax.experimental import pallas as pl
from jax.experimental.pallas import tpu as pltpu
from jax.sharding import PartitionSpec as P

MESH = pl.DeviceIdType.MESH
F32 = jnp.float32
BF16 = jnp.bfloat16

first_decay = 0.9
second_decay = 0.95
adam_epsilon = 1e-08
graft_floor = 1e-06
learn_rate = 0.05

D = 768
ROWS = 96
HALF = 48
COLS = 384
SPLIT = 80
STEP = 16


def row_loop(rows, body):
    def run(i, carry):
        body(pl.ds(pl.multiple_of(i * STEP, STEP), STEP))
        return carry

    lax.fori_loop(0, rows // STEP, run, 0)


def kernel(
    grads, weights, mom_first, mom_second, left_stat, right_stat, left_root, right_root, owners,
    w_out, first_out, second_out, left_out, right_out,
    loc, pair, relay_up, relay_down, from_low, from_high, quads, part2, part3, g,
    root_wide, w_in, first_in, second_in,
    left_bf, left_pick, right_bf, h, piece, slots, picked,
    adam_mine, adam_all, square_mine, square_all,
    send_sem, recv_sem, local_sem,
):
    r = lax.axis_index("rep")
    o = lax.axis_index("own")
    x, z = r // 4, r % 4
    y, c = o // 2, o % 2
    other = 1 - c

    def at_x(d):
        return (((x + d) % 4) * 4 + z, o)

    def at_y(d):
        return (r, ((y + d) % 4) * 2 + c)

    def at_z(d):
        return (x * 4 + (z + d) % 4, o)

    partner = (r, y * 2 + other)
    ring = {"x": at_x, "y": at_y, "z": at_z}
    place = {"x": x, "y": y, "z": z}
    orders = ("yxz", "xzy", "zyx")

    count = [0]

    def send(src, dst, device):
        i = count[0]
        count[0] += 1
        copy = pltpu.make_async_remote_copy(
            src_ref=src, dst_ref=dst, send_sem=send_sem.at[i], recv_sem=recv_sem.at[i],
            device_id=device, device_id_type=MESH,
        )
        copy.start()
        started.append(copy)
        return copy

    started = []
    local_count = [0]

    def fetch(src, dst):
        i = local_count[0]
        local_count[0] += 1
        copy = pltpu.make_async_copy(src, dst, local_sem.at[i])
        copy.start()
        return copy

    def grad_rows(m, k, core):
        j = (place[orders[m][0]] + k) % 4
        start = pl.multiple_of((2 * j + core) * ROWS, ROWS)
        return grads.at[0, 0, m, pl.ds(start, ROWS), :]

    barrier = pltpu.get_barrier_semaphore()
    friends = [(r, (o + k) % 8) for k in range(1, 8)]
    friends += [at_x(k) for k in (1, 2, 3)] + [at_z(k) for k in (1, 2, 3)]
    for friend in friends:
        pl.semaphore_signal(barrier, inc=1, device_id=friend, device_id_type=MESH)

    own_half = {}
    for k in (2, 1, 3, 0):
        for m in range(3):
            own_half[m, k] = fetch(grad_rows(m, k, c), loc.at[m, k])
    pl.semaphore_wait(barrier, len(friends))

    pair_copy = {}
    for k in (2, 1, 3, 0):
        for m in range(3):
            pair_copy[m, k] = send(grad_rows(m, k, other), pair.at[m, k], partner)

    left_copy = fetch(left_root.at[0], root_wide.at[0])
    right_copy = fetch(right_root.at[0], root_wide.at[1])
    left_stat_copy = fetch(left_stat.at[0], left_out.at[0])
    right_stat_copy = fetch(right_stat.at[0], right_out.at[0])
    first_copy = fetch(mom_first, first_in)
    second_copy = fetch(mom_second, second_in)
    weight_copy = fetch(weights, w_in)

    def merge(dst, src, start, rows):
        def body(at):
            at = pl.ds(at.start + start, STEP) if start else at
            dst[at, :] = (dst[at, :].astype(F32) + src[at, :].astype(F32)).astype(BF16)

        row_loop(rows, body)

    def merge_pair(m, k):
        own_half[m, k].wait()
        pair_copy[m, k].wait_recv()
        merge(loc.at[m, k], pair.at[m, k], 0, ROWS)

    top, low = pl.ds(0, HALF), pl.ds(HALF, HALF)
    to_relay = {}
    for m in range(3):
        merge_pair(m, 2)
        ring1 = ring[orders[m][0]]
        to_relay[m, 1] = send(loc.at[m, 2, top], relay_up.at[m], ring1(1))
        to_relay[m, -1] = send(loc.at[m, 2, low], relay_down.at[m], ring1(-1))
    direct = {}
    for m in range(3):
        ring1 = ring[orders[m][0]]
        merge_pair(m, 1)
        direct[m, 1] = send(loc.at[m, 1, low], from_low.at[m, low], ring1(1))
        merge_pair(m, 3)
        direct[m, -1] = send(loc.at[m, 3, top], from_high.at[m, top], ring1(-1))
    relayed = {}
    for m in range(3):
        ring1 = ring[orders[m][0]]
        to_relay[m, 1].wait_recv()
        merge(loc.at[m, 1, top], relay_up.at[m], 0, HALF)
        relayed[m, 1] = send(loc.at[m, 1, top], from_low.at[m, top], ring1(1))
        to_relay[m, -1].wait_recv()
        merge(loc.at[m, 3, low], relay_down.at[m], 0, HALF)
        relayed[m, -1] = send(loc.at[m, 3, low], from_high.at[m, low], ring1(-1))
    for m in range(3):
        own_half[m, 0].wait()
        pair_copy[m, 0].wait_recv()

    left_copy.wait()
    right_copy.wait()

    def narrow(at):
        left_bf[at, :] = root_wide[0, at, :].astype(BF16)
        right_bf[at, :] = root_wide[1, at, :].astype(BF16)

    row_loop(D, narrow)
    for i in range(4):
        for parity, q in ((0, x), (1, z)):
            start = pl.multiple_of((2 * i + parity) * ROWS + HALF * (q // 2), STEP)
            left_pick[parity, pl.ds(HALF * i, HALF), :] = left_bf[pl.ds(start, HALF), :]

    second_ring = {}
    for m in range(3):
        for name in (1, -1):
            direct[m, name].wait_recv()
            relayed[m, name].wait_recv()
        for half in range(2):
            def total(at, m=m, half=half):
                rows = pl.ds(pl.multiple_of(at.start + half * HALF, STEP), STEP)
                value = loc[m, 0, rows, :].astype(F32) + pair[m, 0, rows, :].astype(F32)
                value += from_low[m, rows, :].astype(F32) + from_high[m, rows, :].astype(F32)
                value = value.astype(BF16)
                quads[m, 2 * half, at, :] = value[:, :COLS]
                quads[m, 2 * half + 1, at, :] = value[:, COLS:]

            row_loop(HALF, total)
        ring2, a2 = ring[orders[m][1]], place[orders[m][1]]
        for k in (2, 1, 3):
            second_ring[m, k] = send(quads.at[m, (a2 + k) % 4], part2.at[m, k - 1], ring2(k))

    third_ring = {}
    for m in range(3):
        a2, a3 = place[orders[m][1]], place[orders[m][2]]
        for k in (1, 3, 2):
            second_ring[m, k].wait_recv()

        def total(at, m=m, a2=a2, a3=a3):
            value = quads[m, a2, at, :].astype(F32) + part2[m, 0, at, :].astype(F32)
            value += part2[m, 1, at, :].astype(F32) + part2[m, 2, at, :].astype(F32)
            part3[m, a3, at, :] = value.astype(BF16)

        row_loop(HALF, total)
        ring3 = ring[orders[m][2]]
        for k in (2, 1, 3):
            third_ring[m, k] = send(part3.at[m, a3], part3.at[m, a3], ring3(k))

    def quadrant(m, j, q):
        start = pl.multiple_of((2 * j + c) * ROWS + HALF * (q // 2), STEP)
        return g.at[m, q % 2, pl.ds(start, HALF), :]

    gather2, gather1 = {}, {}

    def spread(m, k):
        ring1, a1, a2 = ring[orders[m][0]], place[orders[m][0]], place[orders[m][1]]
        here = quadrant(m, a1, (a2 - k) % 4)
        for d in (1, -1):
            gather1[m, k, d] = send(here, here, ring1(d))

    for m in range(3):
        a1, a2 = place[orders[m][0]], place[orders[m][1]]
        for k in (1, 3, 2):
            third_ring[m, k].wait_recv()
        here = quadrant(m, a1, a2)

        def total(at, m=m, here=here):
            value = part3[m, 0, at, :].astype(F32) + part3[m, 1, at, :].astype(F32)
            value += part3[m, 2, at, :].astype(F32) + part3[m, 3, at, :].astype(F32)
            here[at, :] = value.astype(BF16)

        row_loop(HALF, total)
        ring2 = ring[orders[m][1]]
        for k in (2, 1, 3):
            gather2[m, k] = send(here, here, ring2(k))
        spread(m, 0)
    for k in (1, 3, 2):
        for m in range(3):
            gather2[m, k].wait_recv()
            spread(m, k)

    shared = {}

    def share(m, k):
        j = (place[orders[m][0]] + k) % 4
        start = pl.multiple_of((2 * j + c) * ROWS, STEP)
        here = g.at[m, :, pl.ds(start, ROWS), :]
        shared[m, k] = send(here, here, partner)

    for m in range(3):
        share(m, 0)
    relay1 = {}
    for k, d in ((0, 1), (3, -1), (1, 1), (2, -1)):
        for m in range(3):
            ring1, a1, a2 = ring[orders[m][0]], place[orders[m][0]], place[orders[m][1]]
            gather1[m, k, d].wait_recv()
            there = quadrant(m, (a1 - d) % 4, (a2 - k) % 4)
            relay1[m, k] = send(there, there, ring1(d))
    for m in range(3):
        for k, d in ((2, 1), (3, 1), (0, -1), (1, -1)):
            gather1[m, k, d].wait_recv()
        share(m, 1)
        share(m, 3)
    for m in range(3):
        for k in range(4):
            relay1[m, k].wait_recv()
        share(m, 2)
    for m in range(3):
        for k in range(4):
            shared[m, k].wait_recv()

    item = jnp.where(owners[1] == o, 1, jnp.where(owners[2] == o, 2, 0))
    holding = jnp.where(owners[0] == o, 1, jnp.where(item > 0, 1, 0)).astype(F32)

    def half_rows(i, carry):
        at = pl.ds(pl.multiple_of(i * 192, 192), 192)
        value = jnp.dot(g[item, 0, at, :], right_bf[:COLS, :], preferred_element_type=F32)
        value += jnp.dot(g[item, 1, at, :], right_bf[COLS:, :], preferred_element_type=F32)
        value = value.astype(BF16)
        h[0, at, :] = value[:, :COLS]
        h[1, at, :] = value[:, COLS:]
        return carry

    lax.fori_loop(0, 4, half_rows, 0)
    for parity, q in ((0, x), (1, z)):
        value = jnp.dot(left_pick[parity], h[q % 2], preferred_element_type=F32).astype(BF16)
        for i in range(4):
            piece[2 * i + parity] = value[HALF * i : HALF * (i + 1), :]
    piece_copy = {}
    for k in range(1, 8):
        p = (o + k) % 8
        piece_copy[k] = send(piece.at[p], slots.at[o], (r, p))
    mine_copy = fetch(piece.at[o], slots.at[o])

    first_copy.wait()
    second_copy.wait()

    def fold(value):
        value = jnp.sum(value, axis=0, keepdims=True)
        return sum(value[:, 128 * i : 128 * (i + 1)] for i in range(value.shape[1] // 128))

    own_rows = pl.multiple_of(o * ROWS, STEP)
    for m in range(3):
        def moment(i, carry, m=m):
            at = pl.ds(pl.multiple_of(i * STEP, STEP), STEP)
            there = pl.ds(pl.multiple_of(own_rows + i * STEP, STEP), STEP)
            for half in range(2):
                cols = pl.ds(COLS * half, COLS)
                grad = g[m, half, there, :].astype(F32)
                first = first_decay * first_in[m, at, cols] + (1.0 - first_decay) * grad
                second = second_decay * second_in[m, at, cols] + (1.0 - second_decay) * grad * grad
                first_out[m, at, cols] = first
                second_out[m, at, cols] = second
                step = first / (jnp.sqrt(second) + adam_epsilon)
                carry = carry + fold(step * step)
            return carry

        total = lax.fori_loop(0, ROWS // STEP, moment, jnp.zeros((1, 128), F32))
        adam_mine[m] = jnp.broadcast_to(total, (8, 128))
    adam_copy = {}
    for k in range(1, 8):
        adam_copy[k] = send(adam_mine, adam_all.at[o], (r, (o + k) % 8))
    adam_local = fetch(adam_mine, adam_all.at[o])

    def square(i, carry):
        at = pl.ds(pl.multiple_of(i * 192, 192), 192)
        for half in range(2):
            value = jnp.dot(left_bf[at, :], h[half], preferred_element_type=F32)
            carry = carry + fold(value * value)
        return carry

    total = lax.fori_loop(0, 4, square, jnp.zeros((1, 128), F32))
    square_mine[...] = jnp.broadcast_to(total, (8, 128))
    square_copy = {}
    for k in range(1, 8):
        square_copy[k] = send(square_mine, square_all.at[o], (r, (o + k) % 8))
    square_local = fetch(square_mine, square_all.at[o])

    for k in range(1, 8):
        piece_copy[k].wait_recv()
    mine_copy.wait()
    a = x + c * (z - x)

    def near(d):
        return (other * (((x + d) % 4) * 4 + z) + c * (x * 4 + (z + d) % 4), o)

    for m in range(3):
        picked[a, pl.ds(HALF * m, HALF), :] = slots[owners[m]]
    upper, lower = pl.ds(0, SPLIT), pl.ds(SPLIT, 3 * HALF - SPLIT)
    update = {}
    for d, part in ((1, upper), (-1, lower), (1, lower), (-1, upper)):
        here = picked.at[a, part]
        update[d, part is upper] = send(here, here, near(d))

    left_stat_copy.wait()

    def left_rows(i, carry):
        at = pl.ds(pl.multiple_of(i * 192, 192), 192)
        dims = (((1,), (1,)), ((), ()))
        value = lax.dot_general(g[item, 0, at, :], g[item, 0], dims, preferred_element_type=F32)
        value += lax.dot_general(g[item, 1, at, :], g[item, 1], dims, preferred_element_type=F32)
        left_out[0, at, :] = left_out[0, at, :] + holding * value
        return carry

    lax.fori_loop(0, 4, left_rows, 0)

    onward = {}
    for d, part in ((1, upper), (-1, lower)):
        update[d, part is upper].wait_recv()
        there = picked.at[(a - d) % 4, part]
        onward[d] = send(there, there, near(d))

    right_stat_copy.wait()
    dims = (((0,), (0,)), ((), ()))
    for i in range(2):
        for j in range(2):
            value = lax.dot_general(g[item, i], g[item, j], dims, preferred_element_type=F32)
            rows, cols = pl.ds(COLS * i, COLS), pl.ds(COLS * j, COLS)
            right_out[0, rows, cols] = right_out[0, rows, cols] + holding * value

    weight_copy.wait()
    for k in range(1, 8):
        adam_copy[k].wait_recv()
        square_copy[k].wait_recv()
    adam_local.wait()
    square_local.wait()
    rates = []
    for m in range(3):
        adam_total = adam_all[0, m, 0:1, :]
        for p in range(1, 8):
            adam_total = adam_total + adam_all[p, m, 0:1, :]
        adam_mean = jnp.sum(adam_total, axis=1, keepdims=True) / (D * D)
        squares = square_all[owners[m]][0:1, :]
        mean = jnp.sum(squares, axis=1, keepdims=True) / (D * D)
        rates.append(learn_rate * jnp.sqrt(adam_mean / (mean + graft_floor)))

    update[1, False].wait_recv()
    update[-1, True].wait_recv()
    onward[1].wait_recv()
    onward[-1].wait_recv()
    for m in range(3):
        for q in range(4):
            rows, cols = pl.ds(HALF * (q // 2), HALF), pl.ds(COLS * (q % 2), COLS)
            value = picked[q, pl.ds(HALF * m, HALF), :].astype(F32)
            w_out[m, rows, cols] = w_in[m, rows, cols] - rates[m] * value

    for copy in started:
        copy.wait_send()


def on_device(
    grads, weights, mom_first, mom_second, left_stat, right_stat, left_root, right_root, owners
):
    rows = jax.ShapeDtypeStruct((3, ROWS, D), F32)
    matrix = jax.ShapeDtypeStruct((1, D, D), F32)
    anywhere = pl.BlockSpec(memory_space=pl.ANY)
    vmem = pl.BlockSpec(memory_space=pltpu.VMEM)
    return pl.pallas_call(
        kernel,
        out_shape=(rows, rows, rows, matrix, matrix),
        in_specs=[anywhere] * 8 + [pl.BlockSpec(memory_space=pltpu.SMEM)],
        out_specs=(vmem,) * 5,
        scratch_shapes=[
            pltpu.VMEM((3, 4, ROWS, D), BF16),
            pltpu.VMEM((3, 4, ROWS, D), BF16),
            pltpu.VMEM((3, HALF, D), BF16),
            pltpu.VMEM((3, HALF, D), BF16),
            pltpu.VMEM((3, ROWS, D), BF16),
            pltpu.VMEM((3, ROWS, D), BF16),
            pltpu.VMEM((3, 4, HALF, COLS), BF16),
            pltpu.VMEM((3, 3, HALF, COLS), BF16),
            pltpu.VMEM((3, 4, HALF, COLS), BF16),
            pltpu.VMEM((3, 2, D, COLS), BF16),
            pltpu.VMEM((2, D, D), F32),
            pltpu.VMEM((3, ROWS, D), F32),
            pltpu.VMEM((3, ROWS, D), F32),
            pltpu.VMEM((3, ROWS, D), F32),
            pltpu.VMEM((D, D), BF16),
            pltpu.VMEM((2, 4 * HALF, D), BF16),
            pltpu.VMEM((D, D), BF16),
            pltpu.VMEM((2, D, COLS), BF16),
            pltpu.VMEM((8, HALF, COLS), BF16),
            pltpu.VMEM((8, HALF, COLS), BF16),
            pltpu.VMEM((4, 3 * HALF, COLS), BF16),
            pltpu.VMEM((3, 8, 128), F32),
            pltpu.VMEM((8, 3, 8, 128), F32),
            pltpu.VMEM((8, 128), F32),
            pltpu.VMEM((8, 8, 128), F32),
            pltpu.SemaphoreType.DMA((160,)),
            pltpu.SemaphoreType.DMA((160,)),
            pltpu.SemaphoreType.DMA((24,)),
        ],
        compiler_params=pltpu.CompilerParams(
            collective_id=0, has_side_effects=True, vmem_limit_bytes=56 * 1024 * 1024
        ),
    )(grads, weights, mom_first, mom_second, left_stat, right_stat, left_root, right_root, owners)


def solution(mesh):
    placed = (
        P("rep", "own", None, None, None),
        P(None, "own", None),
        P(None, "own", None),
        P(None, "own", None),
        P("own", None, None),
        P("own", None, None),
        P("own", None, None),
        P("own", None, None),
        P(),
    )
    return jax.shard_map(
        on_device,
        mesh=mesh,
        in_specs=placed,
        out_specs=(
            P(None, "own", None),
            P(None, "own", None),
            P(None, "own", None),
            P("own", None, None),
            P("own", None, None),
        ),
        check_vma=False,
    )
```

time: 269 us -> 69.8 us (0.26)
  blocking collectives: 126 us -> 0 us
  waiting for transfers between devices: 76.5 us -> 0 us
  Pallas kernels: 0 us -> 60.9 us
  matrix products: 25.4 us -> 0 us
  between operations: 19.4 us -> 0.67 us
  other arithmetic: 17.8 us -> 0 us
  local copies, waits for them, and re-layouts: 3.46 us -> 8.04 us
    psum x2 -> x0, blocking collectives: 126 us -> none  [the longest x1 111 us: on_device(): summed = lax.psum(local_grad, ('rep', 'own')).astype(jnp.bfloat16)]
    psum x1 -> x0, waiting for transfers between devices: 76.5 us -> none  [broadcast(): return lax.psum(jnp.where(mine, shard, jnp.zeros_like(shard)), axis)]
    pallas_call x0 -> x1, Pallas kernels: none -> 60.9 us  [on_device(): pl.pallas_call(kernel, out_shape=(rows, rows, rows, matrix, matrix), in_s...]
    dot_general x4 -> x0, matrix products: 25.4 us -> none  [the longest x1 8.55 us: on_device(): jnp.dot(half_product, right_root[0], precision=lax.Precision.HIGHEST)]
    unnamed x10 -> x13, local copies, waits for them, and re-layouts: 0.03 us -> 8.04 us
    convert_element_type x1 -> x0, other arithmetic: 5.52 us -> none  [on_device(): local_grad = grads[0, 0].astype(jnp.float32)]
    reduce_sum x3 -> x0, other arithmetic: 4.97 us -> none  [the longest x1 3.08 us: on_device(): partial_squares = jnp.sum(adam_step * adam_step, axis=(1, 2))]
    select_n x1 -> x0, other arithmetic: 4.78 us -> none  [broadcast(): return lax.psum(jnp.where(mine, shard, jnp.zeros_like(shard)), axis)]
  transfers between devices with their start and end apart: 1 -> 0, of which waited for: 1 -> 0; matrix products, arithmetic and copies ran while one was open for 4% -> 0% of each run, Pallas kernels for 0% -> 0%
where the time goes in v1:
time: 69.8 us; the launch traced here: 69.6 us
  Pallas kernels  60.9 us (87%)
  local copies, waits for them, and re-layouts  8.04 us (12%)
    pallas_call x1, Pallas kernels, on_device(): pl.pallas_call(kernel, out_shape=(rows, rows, rows, matrix, matrix), in_s...  60.9 us
    unnamed x13, local copies, waits for them, and re-layouts  8.04 us

profile of v1, /device:TPU:1, one launch (start us, length us, event | category | flops | bytes accessed | tf_op | source)
XLA Modules:
  0.0 69.6 jit_solution(9192199025332381896)
XLA Ops:
  0.6 60.9 %shard_map.128 = (f32[3,96,768]{2,1,0:T(8,128)}, f32[3,96,768]{2,1,0:T(8,128)}, f32[3,96,768]{2,1,0:T(8,128)}, f32[1,768,768]{2,1,0:T(8,128)}, f32[1,768,768]{2,1,0:T(8,128)}) custom-call(bf16[1,1,3,768,768]{4,3,2,1,0:T(8,128)(2,1)} %grads.1, f32[3,96,768]{2,1,0:T(8,128)} %weights.1, f32[3,96,768]{2,1,0:T(8,128)} %mom_first.1, f32[3,96,768]{2,1,0:T(8,128)} %mom_second.1, ...), custom_call_target="tpu_custom_call" | custom-call | tf_op jit(solution)/shard_map/pallas_call | solution.py:414
  61.6 0.0 copy-start.3
  61.6 0.0 copy-start.2
  61.6 0.0 copy-start.1
  61.6 2.3 %copy.19 = f32[3,96,768]{2,1,0:T(8,128)} copy(f32[3,96,768]{2,1,0:T(8,128)} %get-tuple-element.10) | data formatting | bytes 1769472
  63.9 0.0 copy-done.3
  63.9 0.9 %copy.20 = f32[3,96,768]{2,1,0:T(8,128)} copy(f32[3,96,768]{2,1,0:T(8,128)S(1)} %copy-done.3) | data formatting | bytes 1769472
  64.8 0.0 copy-done.2
  64.8 0.9 %copy.21 = f32[3,96,768]{2,1,0:T(8,128)} copy(f32[3,96,768]{2,1,0:T(8,128)S(1)} %copy-done.2) | data formatting | bytes 1769472
  65.7 0.0 copy-done.1
  65.7 0.0 copy-start
  65.7 1.4 %copy.22 = f32[1,768,768]{2,1,0:T(8,128)} copy(f32[1,768,768]{2,1,0:T(8,128)S(1)} %copy-done.1) | data formatting | bytes 4718592
  67.1 1.1 %copy-done = f32[1,768,768]{2,1,0:T(8,128)S(1)} copy-done((f32[1,768,768]{2,1,0:T(8,128)S(1)}, f32[1,768,768]{2,1,0:T(8,128)}, u32[]{:S(2)}) %copy-start) | copy-done | bytes 2359320
  68.2 1.4 %copy.23 = f32[1,768,768]{2,1,0:T(8,128)} copy(f32[1,768,768]{2,1,0:T(8,128)S(1)} %copy-done) | data formatting | bytes 4718592
Async XLA Ops:
  61.6 2.3 %copy-start.3 = (f32[3,96,768]{2,1,0:T(8,128)S(1)}, f32[3,96,768]{2,1,0:T(8,128)}, u32[]{:S(2)}) copy-start(f32[3,96,768]{2,1,0:T(8,128)} %get-tuple-element.11) | copy-start | bytes 2654212
  61.6 3.2 %copy-start.2 = (f32[3,96,768]{2,1,0:T(8,128)S(1)}, f32[3,96,768]{2,1,0:T(8,128)}, u32[]{:S(2)}) copy-start(f32[3,96,768]{2,1,0:T(8,128)} %get-tuple-element.12) | copy-start | bytes 2654212
  61.6 4.1 %copy-start.1 = (f32[1,768,768]{2,1,0:T(8,128)S(1)}, f32[1,768,768]{2,1,0:T(8,128)}, u32[]{:S(2)}) copy-start(f32[1,768,768]{2,1,0:T(8,128)} %get-tuple-element.13) | copy-start | bytes 7077892
  65.7 2.5 %copy-start = (f32[1,768,768]{2,1,0:T(8,128)S(1)}, f32[1,768,768]{2,1,0:T(8,128)}, u32[]{:S(2)}) copy-start(f32[1,768,768]{2,1,0:T(8,128)} %get-tuple-element.14) | copy-start | bytes 7077892

commit v2 on v1

--- a/solution.py
+++ b/solution.py
@@ -34,13 +34,13 @@
 
 
 def kernel(
-    grads, weights, mom_first, mom_second, left_stat, right_stat, left_root, right_root, owners,
+    grads, weights, mom_first, mom_second, left_stat, right_stat, left_root, right_root, owners_in,
     w_out, first_out, second_out, left_out, right_out,
     loc, pair, relay_up, relay_down, from_low, from_high, quads, part2, part3, g,
     root_wide, w_in, first_in, second_in,
-    left_bf, left_pick, right_bf, h, piece, slots, picked,
+    left_bf, left_pick, left_rest, right_bf, h, h_rest, piece, slots, picked,
     adam_mine, adam_all, square_mine, square_all,
-    send_sem, recv_sem, local_sem,
+    owners, send_sem, recv_sem, local_sem,
 ):
     r = lax.axis_index("rep")
     o = lax.axis_index("own")
@@ -107,6 +107,7 @@
         for m in range(3):
             pair_copy[m, k] = send(grad_rows(m, k, other), pair.at[m, k], partner)
 
+    owner_copy = fetch(owners_in, owners)
     left_copy = fetch(left_root.at[0], root_wide.at[0])
     right_copy = fetch(right_root.at[0], root_wide.at[1])
     left_stat_copy = fetch(left_stat.at[0], left_out.at[0])
@@ -162,10 +163,13 @@
         right_bf[at, :] = root_wide[1, at, :].astype(BF16)
 
     row_loop(D, narrow)
-    for i in range(4):
-        for parity, q in ((0, x), (1, z)):
+    for parity, q in ((0, x), (1, z)):
+        for i in range(4):
             start = pl.multiple_of((2 * i + parity) * ROWS + HALF * (q // 2), STEP)
-            left_pick[parity, pl.ds(HALF * i, HALF), :] = left_bf[pl.ds(start, HALF), :]
+            wide = root_wide[0, pl.ds(start, HALF), :]
+            high = wide.astype(BF16)
+            left_pick[parity, pl.ds(HALF * i, HALF), :] = high
+            left_rest[parity, pl.ds(HALF * i, HALF), :] = (wide - high.astype(F32)).astype(BF16)
 
     second_ring = {}
     for m in range(3):
@@ -265,6 +269,7 @@
         for k in range(4):
             shared[m, k].wait_recv()
 
+    owner_copy.wait()
     item = jnp.where(owners[1] == o, 1, jnp.where(owners[2] == o, 2, 0))
     holding = jnp.where(owners[0] == o, 1, jnp.where(item > 0, 1, 0)).astype(F32)
 
@@ -272,14 +277,20 @@
         at = pl.ds(pl.multiple_of(i * 192, 192), 192)
         value = jnp.dot(g[item, 0, at, :], right_bf[:COLS, :], preferred_element_type=F32)
         value += jnp.dot(g[item, 1, at, :], right_bf[COLS:, :], preferred_element_type=F32)
-        value = value.astype(BF16)
-        h[0, at, :] = value[:, :COLS]
-        h[1, at, :] = value[:, COLS:]
+        high = value.astype(BF16)
+        rest = (value - high.astype(F32)).astype(BF16)
+        h[0, at, :] = high[:, :COLS]
+        h[1, at, :] = high[:, COLS:]
+        h_rest[0, at, :] = rest[:, :COLS]
+        h_rest[1, at, :] = rest[:, COLS:]
         return carry
 
     lax.fori_loop(0, 4, half_rows, 0)
     for parity, q in ((0, x), (1, z)):
-        value = jnp.dot(left_pick[parity], h[q % 2], preferred_element_type=F32).astype(BF16)
+        value = jnp.dot(left_pick[parity], h[q % 2], preferred_element_type=F32)
+        value += jnp.dot(left_rest[parity], h[q % 2], preferred_element_type=F32)
+        value += jnp.dot(left_pick[parity], h_rest[q % 2], preferred_element_type=F32)
+        value = value.astype(BF16)
         for i in range(4):
             piece[2 * i + parity] = value[HALF * i : HALF * (i + 1), :]
     piece_copy = {}
@@ -404,17 +415,25 @@
         copy.wait_send()
 
 
+def store(*refs):
+    copies = [pltpu.make_async_copy(refs[i], refs[5 + i], refs[10].at[i]) for i in range(5)]
+    for copy in copies:
+        copy.start()
+    for copy in copies:
+        copy.wait()
+
+
 def on_device(
     grads, weights, mom_first, mom_second, left_stat, right_stat, left_root, right_root, owners
 ):
     rows = jax.ShapeDtypeStruct((3, ROWS, D), F32)
     matrix = jax.ShapeDtypeStruct((1, D, D), F32)
-    anywhere = pl.BlockSpec(memory_space=pl.ANY)
+    hbm = pl.BlockSpec(memory_space=pltpu.HBM)
     vmem = pl.BlockSpec(memory_space=pltpu.VMEM)
-    return pl.pallas_call(
+    outs = pl.pallas_call(
         kernel,
-        out_shape=(rows, rows, rows, matrix, matrix),
-        in_specs=[anywhere] * 8 + [pl.BlockSpec(memory_space=pltpu.SMEM)],
+        out_shape=(pltpu.VMEM((3, ROWS, D), F32),) * 3 + (pltpu.VMEM((1, D, D), F32),) * 2,
+        in_specs=[hbm] * 9,
         out_specs=(vmem,) * 5,
         scratch_shapes=[
             pltpu.VMEM((3, 4, ROWS, D), BF16),
@@ -433,7 +452,9 @@
             pltpu.VMEM((3, ROWS, D), F32),
             pltpu.VMEM((D, D), BF16),
             pltpu.VMEM((2, 4 * HALF, D), BF16),
+            pltpu.VMEM((2, 4 * HALF, D), BF16),
             pltpu.VMEM((D, D), BF16),
+            pltpu.VMEM((2, D, COLS), BF16),
             pltpu.VMEM((2, D, COLS), BF16),
             pltpu.VMEM((8, HALF, COLS), BF16),
             pltpu.VMEM((8, HALF, COLS), BF16),
@@ -442,14 +463,23 @@
             pltpu.VMEM((8, 3, 8, 128), F32),
             pltpu.VMEM((8, 128), F32),
             pltpu.VMEM((8, 8, 128), F32),
+            pltpu.SMEM((3,), jnp.int32),
             pltpu.SemaphoreType.DMA((160,)),
             pltpu.SemaphoreType.DMA((160,)),
             pltpu.SemaphoreType.DMA((24,)),
         ],
         compiler_params=pltpu.CompilerParams(
-            collective_id=0, has_side_effects=True, vmem_limit_bytes=56 * 1024 * 1024
+            collective_id=0, has_side_effects=True, vmem_limit_bytes=50 * 1024 * 1024
         ),
     )(grads, weights, mom_first, mom_second, left_stat, right_stat, left_root, right_root, owners)
+    return pl.pallas_call(
+        store,
+        out_shape=(rows, rows, rows, matrix, matrix),
+        in_specs=[vmem] * 5,
+        out_specs=(pl.BlockSpec(memory_space=pl.ANY),) * 5,
+        scratch_shapes=[pltpu.SemaphoreType.DMA((5,))],
+        compiler_params=pltpu.CompilerParams(vmem_limit_bytes=1024 * 1024),
+    )(*outs)
 
 
 def solution(mesh):

time: 69.8 us -> 61.8 us (0.89)
  local copies, waits for them, and re-layouts: 8.04 us -> 0 us
    unnamed x13 -> x0, local copies, waits for them, and re-layouts: 8.04 us -> none
    pallas_call x1 -> x2, Pallas kernels: 60.9 us -> 61.1 us  [the longest x1 58 us: on_device(): pl.pallas_call(kernel, out_shape=(pltpu.VMEM((3, ROWS, D), F32),) * 3 + (...]
where the time goes in v2:
time: 61.8 us; the launch traced here: 61.7 us
  Pallas kernels  61.1 us (99%)
  between operations  0.64 us (1%)
    pallas_call x1, Pallas kernels, on_device(): pl.pallas_call(kernel, out_shape=(pltpu.VMEM((3, ROWS, D), F32),) * 3 + (...  58 us
    pallas_call x1, Pallas kernels, on_device(): pl.pallas_call(store, out_shape=(rows, rows, rows, matrix, matrix), in_sp...  3.1 us

profile of v2, /device:TPU:1, one launch (start us, length us, event | category | flops | bytes accessed | tf_op | source)
XLA Modules:
  0.0 61.7 jit_solution(4536222856146010691)
XLA Ops:
  0.6 58.0 %shard_map.128 = (f32[3,96,768]{2,1,0:T(8,128)S(1)}, f32[3,96,768]{2,1,0:T(8,128)S(1)}, f32[3,96,768]{2,1,0:T(8,128)S(1)}, f32[1,768,768]{2,1,0:T(8,128)S(1)}, f32[1,768,768]{2,1,0:T(8,128)S(1)}) custom-call(bf16[1,1,3,768,768]{4,3,2,1,0:T(8,128)(2,1)} %grads.1, f32[3,96,768]{2,1,0:T(8,128)} %weights.1, f32[3,96,768]{2,1,0:T(8,128)} %mom_first.1, ...), custom_call_target="tpu_custom_call" | custom-call | tf_op jit(solution)/shard_map/pallas_call | solution.py:433
  58.6 3.1 %shard_map.129 = (f32[3,96,768]{2,1,0:T(8,128)}, f32[3,96,768]{2,1,0:T(8,128)}, f32[3,96,768]{2,1,0:T(8,128)}, f32[1,768,768]{2,1,0:T(8,128)}, f32[1,768,768]{2,1,0:T(8,128)}) custom-call(f32[3,96,768]{2,1,0:T(8,128)S(1)} %get-tuple-element.10.refs_0_, f32[3,96,768]{2,1,0:T(8,128)S(1)} %get-tuple-element.11.refs_1_, ...), custom_call_target="tpu_custom_call" | custom-call | tf_op jit(solution)/shard_map/pallas_call | solution.py:475
